TPU v7x, 256 devices: a whole 4x4x8 slice. The times are simulated.
256 devices in a mesh: req: 32 (over z, x), tp: 8 (over y, core).
Axes of the slice: x: 4, y: 4, z: 8, core: 2. Of those that a mesh axis runs over, the one named last changes fastest.
Arguments:
- hidden_in: bfloat16 [192, 64, 3072], P('req', None, 'tp'), may hold values from -3 to 3
- request_order: int32 [192], replicated, may hold values from 0 to 191, as said below
- norm_gain: bfloat16 [3072], replicated, may hold values from 0.099609375 to 1.8984375
- w_query: bfloat16 [3072, 3072], P(None, 'tp'), may hold values from -0.109375 to 0.109375
- key_weight: bfloat16 [3072, 1024], P(None, 'tp'), may hold values from -0.4375 to 0.4375
- value_weight: bfloat16 [3072, 1024], P(None, 'tp'), may hold values from -0.109375 to 0.109375
- w_out: bfloat16 [3072, 3072], P('tp'), may hold values from -0.109375 to 0.109375
- key_cache: bfloat16 [192, 8, 3456, 128], P('req', 'tp'), may hold values from -360 to 360
- cached_values: bfloat16 [192, 8, 3456, 128], P('req', 'tp'), may hold values from -24 to 24
- cache_lengths: int32 [192], P('req'), may hold values from 864 to 3456, as said below
- tree_parent: int32 [192, 64], P('req'), may hold values from 0 to 63, as said below
- kept_nodes: int32 [192, 8], P('req'), may hold values from 0 to 63
Outputs:
- layer_out: bfloat16 [192, 64, 3072], P('req', None, 'tp')
- appended: bfloat16 [192, 2, 8, 8, 128], P('req', None, None, 'tp')
Inputs may be any that keep to these rules, and one draw needn't show every extreme that they name: `request_order`: each request is held by exactly one slot. The 6 requests of one device's rows go to 6 different devices of req, and the slots of one device hold requests of 6 different devices. `cache_lengths`: some slot has exactly 3456 live positions. `tree_parent`: node 0 has parent 0; every other node's parent has a lower index.
All inputs are finite; a program needn't handle non-finite values.
Results may differ from a plain program's by a relative error of at most 0.0085.
The roundings to bfloat16 on the way count: a program that leaves them out, or rounds other values in their place, can miss the bound.
Values may be sent and summed in bfloat16 or wider, within the bound.
A program may use at most 128 MiB of HBM per device.

v0:
```python
import jax
import jax.numpy as jnp
from jax import lax
from jax.sharding import PartitionSpec as P

HEAD_WIDTH = 128
NORM_EPSILON = 1e-05


def rotary_embedding(vectors, token_positions):
    half_dim = vectors.shape[-1] // 2
    frequency = 500000.0 ** (-jnp.arange(half_dim, dtype=jnp.float32) * 2.0 / vectors.shape[-1])
    angles = token_positions[..., None] * frequency
    cosine = jnp.cos(angles)[..., None, :]
    sine = jnp.sin(angles)[..., None, :]
    first_half = vectors[..., :half_dim]
    second_half = vectors[..., half_dim:]
    return jnp.concatenate(
        [first_half * cosine - second_half * sine, second_half * cosine + first_half * sine],
        axis=-1,
    )


def body(
    hidden_in,
    request_order,
    norm_gain,
    w_query,
    key_weight,
    value_weight,
    w_out,
    key_cache,
    cached_values,
    cache_lengths,
    tree_parent,
    kept_nodes,
):
    slots_here = key_cache.shape[0]
    tree_length = hidden_in.shape[1]
    width_local = hidden_in.shape[2]
    local_groups = key_cache.shape[1]
    local_heads = w_query.shape[1] // HEAD_WIDTH
    group_width = local_heads // local_groups
    slot_ids = lax.axis_index("req") * slots_here + jnp.arange(slots_here, dtype=jnp.int32)
    own_order = request_order[slot_ids]
    piece = lax.all_gather(hidden_in, "req", axis=0, tiled=True)
    piece_ids = jnp.arange(piece.shape[0], dtype=jnp.int32)
    chooser = (own_order[:, None] == piece_ids[None, :]).astype(jnp.bfloat16)
    dealt = jnp.einsum("rm,mtd->rtd", chooser, piece, preferred_element_type=jnp.float32).astype(
        jnp.bfloat16
    )
    widened = lax.all_gather(dealt, "tp", axis=2, tiled=True).astype(jnp.float32)
    normalized_input = (
        widened
        * lax.rsqrt(jnp.mean(widened * widened, axis=-1, keepdims=True) + NORM_EPSILON)
        * norm_gain.astype(jnp.float32)
    ).astype(jnp.bfloat16)
    flat_rows = normalized_input.reshape(slots_here * tree_length, normalized_input.shape[2])
    query_rows = jnp.dot(flat_rows, w_query, preferred_element_type=jnp.float32).reshape(
        slots_here, tree_length, local_heads, HEAD_WIDTH
    )
    fresh_keys = jnp.dot(flat_rows, key_weight, preferred_element_type=jnp.float32).reshape(
        slots_here, tree_length, local_groups, HEAD_WIDTH
    )
    fresh_values = (
        jnp.dot(flat_rows, value_weight, preferred_element_type=jnp.float32)
        .astype(jnp.bfloat16)
        .reshape(slots_here, tree_length, local_groups, HEAD_WIDTH)
    )
    node_ids = jnp.arange(tree_length, dtype=jnp.int32)
    parent_link = (
        (tree_parent[:, :, None] == node_ids[None, None, :]) & (node_ids[None, :, None] > 0)
    ).astype(jnp.float32)
    ancestry = jnp.eye(tree_length, dtype=jnp.float32)[None] + parent_link
    for sweep in range(tree_length.bit_length()):
        ancestry = jnp.minimum(
            jnp.einsum("rij,rjk->rik", ancestry, ancestry, precision=lax.Precision.HIGHEST), 1.0
        )
    token_positions = cache_lengths.astype(jnp.float32)[:, None] + jnp.sum(ancestry, axis=-1) - 1.0
    rotated_query = (
        rotary_embedding(query_rows, token_positions)
        .astype(jnp.bfloat16)
        .reshape(slots_here, tree_length, local_groups, group_width, HEAD_WIDTH)
    )
    key_rot = rotary_embedding(fresh_keys, token_positions).astype(jnp.bfloat16)
    score_scale = HEAD_WIDTH ** (-0.5)
    cache_scores = (
        jnp.einsum(
            "rtgqd,rgcd->rgqtc", rotated_query, key_cache, preferred_element_type=jnp.float32
        )
        * score_scale
    )
    live_keys = jnp.arange(key_cache.shape[2], dtype=jnp.int32)[None, :] < cache_lengths[:, None]
    cache_scores = jnp.where(live_keys[:, None, None, None, :], cache_scores, -jnp.inf)
    tree_scores = (
        jnp.einsum("rtgqd,rsgd->rgqts", rotated_query, key_rot, preferred_element_type=jnp.float32)
        * score_scale
    )
    tree_scores = jnp.where(ancestry[:, None, None] > 0, tree_scores, -jnp.inf)
    row_max = jnp.maximum(jnp.max(cache_scores, axis=-1), jnp.max(tree_scores, axis=-1))
    cache_exp = jnp.exp(cache_scores - row_max[..., None])
    tree_exp = jnp.exp(tree_scores - row_max[..., None])
    row_total = jnp.sum(cache_exp, axis=-1) + jnp.sum(tree_exp, axis=-1)
    cache_weights = (cache_exp / row_total[..., None]).astype(jnp.bfloat16)
    tree_weights = (tree_exp / row_total[..., None]).astype(jnp.bfloat16)
    attended = jnp.einsum(
        "rgqtc,rgcd->rtgqd", cache_weights, cached_values, preferred_element_type=jnp.float32
    )
    attended = attended + jnp.einsum(
        "rgqts,rsgd->rtgqd", tree_weights, fresh_values, preferred_element_type=jnp.float32
    )
    attended = attended.astype(jnp.bfloat16).reshape(
        slots_here, tree_length, local_heads * HEAD_WIDTH
    )
    keep_select = (kept_nodes[:, :, None] == node_ids[None, None, :]).astype(jnp.bfloat16)
    stacked = jnp.stack([key_rot, fresh_values], axis=1)
    appended = jnp.einsum(
        "rkt,rxtgd->rxkgd", keep_select, stacked, preferred_element_type=jnp.float32
    ).astype(jnp.bfloat16)
    partials = jnp.dot(
        attended.reshape(-1, attended.shape[2]), w_out, preferred_element_type=jnp.float32
    )
    summed = lax.psum(partials, "tp")
    my_share = lax.dynamic_slice_in_dim(summed, lax.axis_index("tp") * width_local, width_local, 1)
    layer_out = (my_share.reshape(dealt.shape) + dealt.astype(jnp.float32)).astype(jnp.bfloat16)
    return (layer_out, appended)


def solution(mesh):
    placed = (
        P("req", None, "tp"),
        P(),
        P(),
        P(None, "tp"),
        P(None, "tp"),
        P(None, "tp"),
        P("tp", None),
        P("req", "tp", None, None),
        P("req", "tp", None, None),
        P("req"),
        P("req", None),
        P("req", None),
    )
    return jax.shard_map(
        body,
        mesh=mesh,
        in_specs=placed,
        out_specs=(P("req", None, "tp"), P("req", None, None, "tp", None)),
        check_vma=False,
    )
```

profile of v0, /device:TPU:2, one launch (start us, length us, event | category | flops | bytes accessed | tf_op | source)
XLA Modules:
  0.0 284.8 jit_solution(10960639715566622475)
XLA Ops:
  7.2 0.0 copy-start
  7.2 0.0 all-gather.3.cloned.1.call-start
  7.2 0.7 all-gather.3.cloned.1.call-update
  7.9 0.0 all-gather.5.cloned.1.call-start
  8.0 1.3 gather_fusion
  9.3 0.0 copy-start.4
  9.3 0.0 copy-start.3
  9.3 0.0 copy-start.5
  9.3 106.1 %all-gather.3.cloned.1.call-done = bf16[192,64,384]{2,1,0:T(8,128)(2,1)} async-done(((bf16[6,64,384]{2,1,0:T(8,128)(2,1)}), bf16[192,64,384]{2,1,0:T(8,128)(2,1)}) %all-gather.3.cloned.1.call-update) | async-done | bytes 9437200 | tf_op jit(solution)/shard_map/all_gather | solution.py:46
  115.4 11.9 %fusion.3 = bf16[6,64,384]{2,0,1:T(8,128)(2,1)S(1)} fusion(bf16[192,64,384]{2,1,0:T(8,128)(2,1)} %all-gather.3.cloned.1.call-done, s32[6]{0:T(128)S(1)} %gather_fusion), kind=kOutput, calls=%fused_computation.7 | convolution fusion | flops 56624256 | bytes 9732120 | tf_op jit(solution)/shard_map/rm,mtd->rtd/dot_general | solution.py:49
  127.3 0.8 copy.78
  128.1 0.0 all-gather.5.cloned.1.call-update
  128.1 0.0 all-reduce.2.cloned.1.call-start
  128.2 0.0 copy-done.4
  128.2 0.0 copy-done.3
  128.2 0.0 copy-done.5
  128.3 0.5 convolution_minimum_fusion.6
  128.7 0.3 convolution_minimum_fusion.5
  129.0 0.3 convolution_minimum_fusion.4
  129.4 0.3 convolution_minimum_fusion.3
  129.7 0.3 convolution_minimum_fusion.2
  130.0 0.3 convolution_minimum_fusion.1
  130.4 0.4 fusion.63
  130.8 0.1 copy.54
  131.0 4.5 %copy.51 = bf16[3072,384]{0,1:T(8,128)(2,1)} copy(bf16[3072,384]{1,0:T(8,128)(2,1)} %param.15) | data formatting | bytes 4718592 | tf_op args[3]
  135.5 0.1 add_add_fusion
  135.5 0.8 multiply_cosine_fusion.1
  136.3 0.1 iota_compare_fusion.1
  136.4 19.0 %all-gather.5.cloned.1.call-done = bf16[6,64,3072]{2,1,0:T(8,128)(2,1)} async-done(((bf16[6,64,384]{2,1,0:T(8,128)(2,1)}), bf16[6,64,3072]{2,1,0:T(8,128)(2,1)}) %all-gather.5.cloned.1.call-update) | async-done | bytes 2359312 | tf_op jit(solution)/shard_map/all_gather | solution.py:52
  155.4 0.0 copy-start.2
  155.4 0.0 copy-start.1
  155.4 2.4 fusion.11
  157.7 2.4 fusion.13
  160.2 0.0 copy-done.2
  160.2 0.0 slice-start
  160.2 0.8 convolution_bitcast_fusion
  161.0 0.8 fusion.38
  161.8 0.0 copy-done.1
  161.8 0.0 slice-start.1
  161.8 1.4 fusion.14
  163.2 0.3 subtract_convert_fusion
  163.6 0.0 slice-done
  163.6 0.0 slice-done.1
  163.6 6.9 %fusion.2 = (f32[6,3,64]{2,1,0:T(4,128)S(1)}, f32[6,64,3,3456]{3,1,2,0:T(8,128)}) fusion(pred[6,3456]{1,0:T(8,128)(4,1)S(1)} %iota_compare_fusion.1, bf16[6,1,3456,128]{3,2,1,0:T(8,128)(2,1)S(1)} %bitcast.146, bf16[6,64,3,64]{3,1,2,0:T(8,128)(2,1)S(1)} %get-tuple-element.11, bf16[6,64,3,64]{3,1,2,0:T(8,128)(2,1)S(1)} %get-tuple-element.10), kind=kOutput, calls=%fused_computation.6 | convolution fusion | flops 1031748480 | bytes 21553920 | tf_op jit(solution)/shard_map/rtgqd,rgcd->rgqtc/dot_general | solution.py:88
  170.5 0.4 fusion.64
  171.0 0.1 fusion.27
  171.1 9.2 %fusion.1 = f32[6,3,64]{2,1,0:T(4,128)S(1)} fusion(f32[6,64,3,3456]{3,1,2,0:T(8,128)} %get-tuple-element.19, f32[6,3,64]{2,1,0:T(4,128)S(1)} %max.9, pred[6,3456]{1,0:T(8,128)(4,1)S(1)} %iota_compare_fusion.1), kind=kLoop, calls=%fused_computation.5 | loop fusion | flops 15924096 | bytes 15955200 | tf_op jit(solution)/shard_map/reduce_sum | solution.py:103
  180.3 1.9 convolution_convert_fusion
  182.2 10.3 %fusion.17 = f32[6,128,3,64]{1,3,2,0:T(8,128)S(1)} fusion(bf16[6,1,3456,128]{3,2,1,0:T(8,128)(2,1)} %param.20, f32[6,3,64]{2,1,0:T(4,128)S(1)} %add.98, f32[6,3,64]{2,1,0:T(4,128)S(1)} %max.9, f32[6,64,3,3456]{3,1,2,0:T(8,128)} %get-tuple-element.19, pred[6,3456]{1,0:T(8,128)(4,1)S(1)} %iota_compare_fusion.1), kind=kOutput, calls=%fused_computation.25 | convolution fusion | flops 1039122432 | bytes 21853440 | tf_op jit(solution)/shard_map/rgqtc,rgcd->rtgqd/dot_general | solution.py:106
  192.5 0.3 fusion.24
  192.8 0.3 copy.56
  193.1 0.0 copy-done
  193.1 0.0 copy-start.6
  193.1 3.5 %fusion.28 = f32[384,3072]{1,0:T(8,128)} fusion(bf16[384,3072]{1,0:T(8,128)(2,1)S(1)} %copy-done, bf16[48,8,3,128]{3,2,1,0:T(4,128)(2,1)S(1)} %bitcast.149), kind=kOutput, calls=%fused_computation.48 | convolution fusion | flops 905969664 | bytes 7372800 | tf_op jit(solution)/shard_map/dot_general | solution.py:120
  196.7 0.0 all-reduce.2.cloned.1.call-update
  196.7 0.0 copy-done.6
  196.7 0.8 fusion.25
  197.5 78.8 %all-reduce.2.cloned.1.call-done = f32[384,3072]{1,0:T(8,128)} async-done(((f32[384,3072]{1,0:T(8,128)}), f32[384,3072]{1,0:T(8,128)}) %all-reduce.2.cloned.1.call-update) | async-done | bytes 4718608 | tf_op jit(solution)/shard_map/psum | solution.py:123
  276.3 1.1 constant_dynamic-slice_fusion
  277.4 0.8 add_convert_fusion
  (12 shorter events, 0.1 us)
Async XLA Ops:
  7.2 185.9 %copy-start = (bf16[384,3072]{1,0:T(8,128)(2,1)S(1)}, bf16[384,3072]{1,0:T(8,128)(2,1)}, u32[]{:S(2)}) copy-start(bf16[384,3072]{1,0:T(8,128)(2,1)} %param.18) | copy-start | bytes 7077892
  7.2 108.2 %all-gather.3.cloned.1.call-start = ((), (), s32[]{:S(2)}) async-start(), calls=%async_computation | async-start | bytes 9732096 | tf_op jit(solution)/shard_map/all_gather | solution.py:46
  7.9 147.5 %all-gather.5.cloned.1.call-start = ((), (), s32[]{:S(2)}) async-start(), calls=%async_computation.1 | async-start | bytes 2654208 | tf_op jit(solution)/shard_map/all_gather | solution.py:52
  9.3 118.9 %copy-start.4 = (s32[6]{0:T(128)S(1)}, s32[6]{0:T(128)}, u32[]{:S(2)}) copy-start(s32[6]{0:T(128)} %param.21) | copy-start | bytes 76
  9.3 118.9 %copy-start.3 = (bf16[3072]{0:T(1024)(128)(2,1)S(1)}, bf16[3072]{0:T(1024)(128)(2,1)}, u32[]{:S(2)}) copy-start(bf16[3072]{0:T(1024)(128)(2,1)} %param.14) | copy-start | bytes 18436
  9.3 118.9 %copy-start.5 = (s32[6,64]{1,0:T(8,128)S(1)}, s32[6,64]{1,0:T(8,128)}, u32[]{:S(2)}) copy-start(s32[6,64]{1,0:T(8,128)} %param.22) | copy-start | bytes 4612
  128.1 148.2 %all-reduce.2.cloned.1.call-start = ((), (), s32[]{:S(2)}) async-start(), calls=%async_computation.2 | async-start | bytes 9437184 | tf_op jit(solution)/shard_map/psum | solution.py:123
  155.4 4.8 %copy-start.2 = (bf16[3072,128]{1,0:T(8,128)(2,1)S(1)}, bf16[3072,128]{1,0:T(8,128)(2,1)}, u32[]{:S(2)}) copy-start(bf16[3072,128]{1,0:T(8,128)(2,1)} %param.16) | copy-start | bytes 2359300
  155.4 6.4 %copy-start.1 = (bf16[3072,384]{0,1:T(8,128)(2,1)S(1)}, bf16[3072,384]{0,1:T(8,128)(2,1)}, u32[]{:S(2)}) copy-start(bf16[3072,384]{0,1:T(8,128)(2,1)} %copy.51) | copy-start | bytes 7077892
  160.2 3.4 %slice-start = ((s8[5308416]{0:T(1024)(128)(4,1)}), s8[4194304]{0:T(1024)(128)(4,1)S(1)}, s32[]{:S(2)}) async-start(s8[5308416]{0:T(1024)(128)(4,1)} %bitcast.145), calls=%async_computation.3 | async-start | bytes 8388608
  161.8 1.7 slice-start.1
  193.1 3.6 %copy-start.6 = (s32[6,8]{1,0:T(8,128)S(1)}, s32[6,8]{1,0:T(8,128)}, u32[]{:S(2)}) copy-start(s32[6,8]{1,0:T(8,128)} %param.23) | copy-start | bytes 580
Sparse Core Ops, SparseCore 0:
  10.6 104.8 all-gather.2
  128.2 27.0 all-gather.4
  196.8 79.4 all-reduce.1
where the time goes:
time: 285 us
  waiting for transfers between devices  205 us (72%)
  matrix products  40.8 us (14%)
  other arithmetic  17 us (6%)
  between operations  14.1 us (5%)
  local copies, waits for them, and re-layouts  8.1 us (3%)
    all_gather x1, waiting for transfers between devices, body(): piece = lax.all_gather(hidden_in, 'req', axis=0, tiled=True)  106 us
    psum x1, waiting for transfers between devices, body(): summed = lax.psum(partials, 'tp')  78.8 us
    all_gather x1, waiting for transfers between devices, body(): lax.all_gather(dealt, 'tp', axis=2, tiled=True).astype(jnp.float32)  19 us
    dot_general x1, matrix products, body(): jnp.einsum('rm,mtd->rtd', chooser, piece, preferred_element_type=jnp.floa...  11.9 us
    dot_general x1, matrix products, body(): jnp.einsum('rgqtc,rgcd->rtgqd', cache_weights, cached_values, preferred_e...  10.3 us
    reduce_sum x2, other arithmetic, body(): row_total = jnp.sum(cache_exp, axis=-1) + jnp.sum(tree_exp, axis=-1)  9.32 us
    dot_general x1, matrix products, body(): jnp.einsum('rtgqd,rgcd->rgqtc', rotated_query, key_cache, preferred_eleme...  6.91 us
  transfers between devices with their start and end apart: 3, of which 3 were waited for; matrix products, arithmetic and copies ran while one was open for 4% of the time, Pallas kernels for 0%

commit v1 on v0

--- a/solution.py
+++ b/solution.py
@@ -1,3 +1,4 @@
+import functools
 import jax
 import jax.numpy as jnp
 from jax import lax
@@ -5,6 +6,38 @@
 
 HEAD_WIDTH = 128
 NORM_EPSILON = 1e-05
+
+
+def shape_body(xs, dimension_no):
+    r2 = list(xs.shape[1:])
+    r2[dimension_no] *= xs.shape[0]
+    kept_arr = jnp.moveaxis(xs, 0, dimension_no).reshape(r2)
+    return kept_arr
+
+
+def answer_the_levels_all(vals, axis_key, array_axis):
+    world_n = lax.axis_size(axis_key)
+    pile = tuple(((m, (m + 1) % world_n) for m in range(world_n)))
+    p_next, x_now = ([], [])
+    t = 0
+    by_place = tuple(((jj, nth) for nth, jj in pile))
+    while t < world_n - 1:
+        if t % 2 == 0:
+            p_next.append(
+                lax.ppermute(p_next[-1] if p_next else vals, axis_name=axis_key, perm=pile)
+            )
+        else:
+            arr_now = lax.ppermute(x_now[-1] if x_now else vals, axis_name=axis_key, perm=by_place)
+            x_now.append(arr_now)
+        t += 1
+    w2 = jnp.stack([*p_next[::-1], vals, *x_now], axis=0)
+    main = lax.axis_index(axis_key) - len(p_next)
+    w2 = w2[(jnp.arange(world_n) - main) % world_n]
+    y = shape_body(w2, array_axis)
+    return y
+
+
+targets_place = functools.partial(answer_the_levels_all, axis_key="tp", array_axis=2)
 
 
 def rotary_embedding(vectors, token_positions):
@@ -49,7 +82,7 @@
     dealt = jnp.einsum("rm,mtd->rtd", chooser, piece, preferred_element_type=jnp.float32).astype(
         jnp.bfloat16
     )
-    widened = lax.all_gather(dealt, "tp", axis=2, tiled=True).astype(jnp.float32)
+    widened = targets_place(dealt).astype(jnp.float32)
     normalized_input = (
         widened
         * lax.rsqrt(jnp.mean(widened * widened, axis=-1, keepdims=True) + NORM_EPSILON)

time: 285 us -> 333 us (1.17)
  local copies, waits for them, and re-layouts: 8.1 us -> 48.4 us
  starting transfers between devices: 0.12 us -> 9.28 us
  waiting for transfers between devices: 205 us -> 197 us
  other arithmetic: 17 us -> 21.5 us
    all_gather x1 -> x0, waiting for transfers between devices: 19 us -> none  [body(): lax.all_gather(dealt, 'tp', axis=2, tiled=True).astype(jnp.float32)]
    ppermute x0 -> x7, waiting for transfers between devices: none -> 18.7 us  [the longest x4 11.4 us: answer_the_levels_all(): lax.ppermute(p_next[-1] if p_next else vals, axis_name=axis_key, perm=pile)]
    convert_element_type x0 -> x3, local copies, waits for them, and re-layouts: none -> 18.4 us  [the longest x2 13.5 us: body(): widened = targets_place(dealt).astype(jnp.float32)]
    unnamed x19 -> x36, local copies, waits for them, and re-layouts: 4.52 us -> 18.7 us
    ppermute x0 -> x7, starting transfers between devices: none -> 9.21 us  [the longest x3 9.2 us: answer_the_levels_all(): lax.ppermute(x_now[-1] if x_now else vals, axis_name=axis_key, perm=by_pl...]
    gather x0 -> x1, local copies, waits for them, and re-layouts: none -> 4.59 us  [answer_the_levels_all(): w2 = w2[(jnp.arange(world_n) - main) % world_n]]
    psum x1, waiting for transfers between devices: 78.8 us -> 74.6 us  [body(): summed = lax.psum(partials, 'tp')]
  transfers between devices with their start and end apart: 3 -> 9, of which waited for: 3 -> 8; matrix products, arithmetic and copies ran while one was open for 4% -> 6% of each run, Pallas kernels for 0% -> 0%
where the time goes in v1:
time: 333 us
  waiting for transfers between devices  197 us (59%)
  local copies, waits for them, and re-layouts  48.4 us (15%)
  matrix products  42 us (13%)
  other arithmetic  21.5 us (6%)
  between operations  14.5 us (4%)
  starting transfers between devices  9.28 us (3%)
    all_gather x1, waiting for transfers between devices, body(): piece = lax.all_gather(hidden_in, 'req', axis=0, tiled=True)  103 us
    psum x1, waiting for transfers between devices, body(): summed = lax.psum(partials, 'tp')  74.6 us
    unnamed x36, local copies, waits for them, and re-layouts  18.7 us
    convert_element_type x2, local copies, waits for them, and re-layouts, body(): widened = targets_place(dealt).astype(jnp.float32)  13.5 us
    dot_general x1, matrix products, body(): jnp.einsum('rm,mtd->rtd', chooser, piece, preferred_element_type=jnp.floa...  11.9 us
    ppermute x4, waiting for transfers between devices, answer_the_levels_all(): lax.ppermute(p_next[-1] if p_next else vals, axis_name=axis_key, perm=pile)  11.4 us
    dot_general x1, matrix products, body(): jnp.einsum('rgqtc,rgcd->rtgqd', cache_weights, cached_values, preferred_e...  10.5 us
    reduce_sum x2, other arithmetic, body(): row_total = jnp.sum(cache_exp, axis=-1) + jnp.sum(tree_exp, axis=-1)  9.38 us
  transfers between devices with their start and end apart: 9, of which 8 were waited for; matrix products, arithmetic and copies ran while one was open for 6% of the time, Pallas kernels for 0%

profile of v1, /device:TPU:2, one launch (start us, length us, event | category | flops | bytes accessed | tf_op | source)
XLA Modules:
  0.0 332.6 jit_solution(4142107959869707690)
XLA Ops:
  7.2 0.7 all-gather.2.cloned.1.call-update
  7.9 0.0 all-reduce.2.cloned.1.call-start
  8.0 1.3 gather_fusion
  9.3 1.2 convolution_minimum_fusion.6
  10.6 0.3 convolution_minimum_fusion.5
  10.9 0.3 convolution_minimum_fusion.4
  11.2 0.3 convolution_minimum_fusion.3
  11.5 0.3 convolution_minimum_fusion.2
  11.9 0.7 iota_compare_fusion.1
  12.6 102.8 %all-gather.2.cloned.1.call-done = bf16[192,64,384]{2,1,0:T(8,128)(2,1)} async-done(((bf16[6,64,384]{2,1,0:T(8,128)(2,1)}), bf16[192,64,384]{2,1,0:T(8,128)(2,1)}) %all-gather.2.cloned.1.call-update) | async-done | bytes 9437200 | tf_op jit(solution)/shard_map/all_gather | solution.py:79
  115.4 11.9 %fusion.29 = bf16[6,64,384]{2,0,1:T(8,128)(2,1)S(1)} fusion(bf16[192,64,384]{2,1,0:T(8,128)(2,1)} %all-gather.2.cloned.1.call-done, s32[6]{0:T(128)S(1)} %gather_fusion), kind=kOutput, calls=%fused_computation.37 | convolution fusion | flops 56771712 | bytes 9732120 | tf_op jit(solution)/shard_map/rm,mtd->rtd/dot_general | solution.py:82
  127.3 0.3 convolution_minimum_fusion.1
  127.7 0.4 fusion.78
  128.2 7.7 %collective-permute-done = bf16[6,64,384]{2,0,1:T(8,128)(2,1)} collective-permute-done((bf16[6,64,384]{2,0,1:T(8,128)(2,1)S(1)}, bf16[6,64,384]{2,0,1:T(8,128)(2,1)}, u32[]{:S(2)}, u32[]{:S(2)}) %collective-permute-start) | collective-permute-done | bytes 294944 | tf_op jit(solution)/shard_map/ppermute | solution.py:27
  135.9 0.1 copy.58
  136.1 4.5 %copy.55 = bf16[3072,384]{0,1:T(8,128)(2,1)} copy(bf16[3072,384]{1,0:T(8,128)(2,1)} %param.15) | data formatting | bytes 4718592 | tf_op args[3]
  140.5 3.0 collective-permute-start.4
  143.5 1.1 collective-permute-done.1
  144.6 0.1 add_add_fusion
  144.7 4.1 %collective-permute-done.4 = bf16[6,64,384]{2,0,1:T(8,128)(2,1)S(1)} collective-permute-done((bf16[6,64,384]{2,0,1:T(8,128)(2,1)S(1)}, bf16[6,64,384]{2,0,1:T(8,128)(2,1)S(1)}, u32[]{:S(2)}, u32[]{:S(2)}) %collective-permute-start.4) | collective-permute-done | bytes 294944 | tf_op jit(solution)/shard_map/ppermute | solution.py:30
  148.8 3.1 collective-permute-start.5
  151.9 1.3 collective-permute-done.2
  153.2 0.8 multiply_cosine_fusion.1
  154.0 3.2 collective-permute-done.5
  157.2 3.1 collective-permute-start.6
  160.3 1.3 collective-permute-done.3
  161.6 0.8 bitcast_dynamic-update-slice_fusion.7
  162.4 0.8 bitcast_dynamic-update-slice_fusion.6
  163.2 1.8 bitcast_dynamic-update-slice_fusion.5
  165.0 1.8 bitcast_dynamic-update-slice_fusion.4
  166.8 0.8 bitcast_dynamic-update-slice_fusion.3
  167.6 0.8 bitcast_dynamic-update-slice_fusion.2
  168.4 0.8 bitcast_dynamic-update-slice_fusion.1
  169.1 0.8 bitcast_dynamic-update-slice_fusion
  170.0 4.6 %gather_fusion.1 = bf16[8,6,64,384]{3,1,2,0:T(8,128)(2,1)} fusion(bf16[8,6,64,384]{3,1,2,0:T(8,128)(2,1)} %bitcast_dynamic-update-slice_fusion, s32[1024]{0:T(1024)S(1)} %pad_clamp_fusion), kind=kCustom, calls=%fused_computation.1 | custom fusion | bytes 4718624 | tf_op jit(solution)/shard_map/gather | solution.py:35
  174.5 2.8 fusion.8
  177.3 0.1 copy.52
  177.4 0.1 rsqrt.13
  177.5 0.1 copy.53
  177.6 5.1 %convert_bitcast_fusion = f32[6,64,8,384]{3,0,1,2:T(8,128)} fusion(bf16[8,6,64,384]{3,1,2,0:T(8,128)(2,1)} %gather_fusion.1), kind=kLoop, calls=%fused_computation.8 | loop fusion | flops 1179648 | bytes 7077888 | tf_op jit(solution)/shard_map/convert_element_type | solution.py:85
  182.7 1.0 fusion.14
  183.8 2.9 copy.54
  186.6 4.9 %reshape.362 = bf16[6,64,3072,1]{2,1,0,3:T(8,128)(2,1)} reshape(bf16[6,64,8,384]{3,2,1,0:T(8,128)(2,1)} %copy.54) | data formatting | bytes 4718592 | tf_op jit(solution)/shard_map/convert_element_type | solution.py:90
  191.5 7.7 %copy.59 = f32[6,64,8,384]{3,2,1,0:T(8,128)} copy(f32[6,64,8,384]{3,0,1,2:T(8,128)} %convert_bitcast_fusion) | data formatting | bytes 9437184 | tf_op jit(solution)/shard_map/convert_element_type | solution.py:85
  199.3 5.8 %reshape.343 = f32[6,64,3072]{2,1,0:T(8,128)} reshape(f32[6,64,8,384]{3,2,1,0:T(8,128)} %copy.59) | data formatting | bytes 9437184 | tf_op jit(solution)/shard_map/convert_element_type | solution.py:85
  205.1 5.9 %copy.76 = f32[48,8,8,384]{3,1,2,0:T(8,128)} copy(f32[48,8,8,384]{3,2,1,0:T(8,128)} %bitcast.168) | data formatting | bytes 9437184
  210.9 2.1 fusion.35
  213.1 0.8 fusion.51
  213.9 1.4 fusion.17
  215.3 0.3 subtract_convert_fusion
  215.7 6.9 %fusion.2 = (f32[6,3,64]{2,1,0:T(4,128)S(1)}, f32[6,64,3,3456]{3,1,2,0:T(8,128)}) fusion(pred[6,3456]{1,0:T(8,128)(4,1)S(1)} %iota_compare_fusion.1, bf16[6,1,3456,128]{3,2,1,0:T(8,128)(2,1)S(1)} %bitcast.173, bf16[6,64,3,64]{3,1,2,0:T(8,128)(2,1)S(1)} %get-tuple-element.11, bf16[6,64,3,64]{3,1,2,0:T(8,128)(2,1)S(1)} %get-tuple-element.10), kind=kOutput, calls=%fused_computation.7 | convolution fusion | flops 1031748480 | bytes 21553920 | tf_op jit(solution)/shard_map/rtgqd,rgcd->rgqtc/dot_general | solution.py:121
  222.5 0.4 fusion.79
  223.0 0.1 fusion.40
  223.1 9.2 %fusion.1 = f32[6,3,64]{2,1,0:T(4,128)S(1)} fusion(f32[6,64,3,3456]{3,1,2,0:T(8,128)} %get-tuple-element.19, f32[6,3,64]{2,1,0:T(4,128)S(1)} %max.9, pred[6,3456]{1,0:T(8,128)(4,1)S(1)} %iota_compare_fusion.1), kind=kLoop, calls=%fused_computation.6 | loop fusion | flops 15924096 | bytes 15955200 | tf_op jit(solution)/shard_map/reduce_sum | solution.py:136
  232.4 10.5 %fusion.24 = f32[6,128,3,64]{1,3,2,0:T(8,128)S(1)} fusion(bf16[6,1,3456,128]{3,2,1,0:T(8,128)(2,1)} %param.20, f32[6,3,64]{2,1,0:T(4,128)S(1)} %add.126, f32[6,3,64]{2,1,0:T(4,128)S(1)} %max.9, f32[6,64,3,3456]{3,1,2,0:T(8,128)} %get-tuple-element.19, pred[6,3456]{1,0:T(8,128)(4,1)S(1)} %iota_compare_fusion.1), kind=kOutput, calls=%fused_computation.36 | convolution fusion | flops 1039122432 | bytes 21853440 | tf_op jit(solution)/shard_map/rgqtc,rgcd->rtgqd/dot_general | solution.py:139
  243.0 0.8 fusion.36
  243.8 0.3 fusion.34
  244.1 0.3 copy.62
  244.4 3.6 %fusion.41 = f32[384,3072]{1,0:T(8,128)} fusion(bf16[384,3072]{1,0:T(8,128)(2,1)S(1)} %copy-done, bf16[48,8,3,128]{3,2,1,0:T(4,128)(2,1)S(1)} %bitcast.176), kind=kOutput, calls=%fused_computation.68 | convolution fusion | flops 905969664 | bytes 7372800 | tf_op jit(solution)/shard_map/dot_general | solution.py:153
  248.0 0.8 fusion.37
  248.9 74.6 %all-reduce.2.cloned.1.call-done = f32[384,3072]{1,0:T(8,128)} async-done(((f32[384,3072]{1,0:T(8,128)}), f32[384,3072]{1,0:T(8,128)}) %all-reduce.2.cloned.1.call-update) | async-done | bytes 4718608 | tf_op jit(solution)/shard_map/psum | solution.py:156
  323.5 1.1 constant_dynamic-slice_fusion
  324.6 0.4 fusion.39
  325.0 0.8 copy.65
  (49 shorter events, 0.3 us)
Async XLA Ops:
  7.2 237.2 %copy-start = (bf16[384,3072]{1,0:T(8,128)(2,1)S(1)}, bf16[384,3072]{1,0:T(8,128)(2,1)}, u32[]{:S(2)}) copy-start(bf16[384,3072]{1,0:T(8,128)(2,1)} %param.18) | copy-start | bytes 7077892
  7.2 108.2 %all-gather.2.cloned.1.call-start = ((), (), s32[]{:S(2)}) async-start(), calls=%async_computation | async-start | bytes 9732096 | tf_op jit(solution)/shard_map/all_gather | solution.py:79
  7.9 315.6 %all-reduce.2.cloned.1.call-start = ((), (), s32[]{:S(2)}) async-start(), calls=%async_computation.1 | async-start | bytes 9437184 | tf_op jit(solution)/shard_map/psum | solution.py:156
  12.6 115.1 %copy-start.7 = (s32[6]{0:T(128)S(1)}, s32[6]{0:T(128)}, u32[]{:S(2)}) copy-start(s32[6]{0:T(128)} %param.21) | copy-start | bytes 76
  12.6 115.1 %copy-start.6 = (bf16[3072]{0:T(1024)(128)(2,1)S(1)}, bf16[3072]{0:T(1024)(128)(2,1)}, u32[]{:S(2)}) copy-start(bf16[3072]{0:T(1024)(128)(2,1)} %param.14) | copy-start | bytes 18436
  127.3 8.5 %collective-permute-start = (bf16[6,64,384]{2,0,1:T(8,128)(2,1)S(1)}, bf16[6,64,384]{2,0,1:T(8,128)(2,1)}, u32[]{:S(2)}, u32[]{:S(2)}) collective-permute-start(bf16[6,64,384]{2,0,1:T(8,128)(2,1)S(1)} %fusion.29), channel_id=1, source_target_pairs={{0,1},{1,2},{2,3},{3,4},{4,5},{5,6},{6,7},{7,0},{8,9},{9,10},{10,1... | collective-permute-start | bytes 884744 | tf_op jit(solution)/shard_map/ppermute | solution.py:27
  135.9 8.7 %collective-permute-start.1 = (bf16[6,64,384]{2,0,1:T(8,128)(2,1)}, bf16[6,64,384]{2,0,1:T(8,128)(2,1)}, u32[]{:S(2)}, u32[]{:S(2)}) collective-permute-start(bf16[6,64,384]{2,0,1:T(8,128)(2,1)} %collective-permute-done), channel_id=1, source_target_pairs={{0,1},{1,2},{2,3},{3,4},{4,5},{5,6},{6,7},{7,0},{8,9},{9,10},{10,1... | collective-permute-start | bytes 884744 | tf_op jit(solution)/shard_map/ppermute | solution.py:27
  140.5 8.3 %collective-permute-start.4 = (bf16[6,64,384]{2,0,1:T(8,128)(2,1)S(1)}, bf16[6,64,384]{2,0,1:T(8,128)(2,1)S(1)}, u32[]{:S(2)}, u32[]{:S(2)}) collective-permute-start(bf16[6,64,384]{2,0,1:T(8,128)(2,1)S(1)} %fusion.29), channel_id=1, source_target_pairs={{1,0},{2,1},{3,2},{4,3},{5,4},{6,5},{7,6},{0,7},{9,8},{10,9},{11,1... | collective-permute-start | bytes 884744 | tf_op jit(solution)/shard_map/ppermute | solution.py:30
  144.6 8.6 %collective-permute-start.2 = (bf16[6,64,384]{2,0,1:T(8,128)(2,1)}, bf16[6,64,384]{2,0,1:T(8,128)(2,1)S(1)}, u32[]{:S(2)}, u32[]{:S(2)}) collective-permute-start(bf16[6,64,384]{2,0,1:T(8,128)(2,1)} %collective-permute-done.1), channel_id=1, source_target_pairs={{0,1},{1,2},{2,3},{3,4},{4,5},{5,6},{6,7},{7,0},{8,9},{9,10},{10,1... | collective-permute-start | bytes 884744 | tf_op jit(solution)/shard_map/ppermute | solution.py:27
  148.8 8.4 %collective-permute-start.5 = (bf16[6,64,384]{2,0,1:T(8,128)(2,1)S(1)}, bf16[6,64,384]{2,0,1:T(8,128)(2,1)S(1)}, u32[]{:S(2)}, u32[]{:S(2)}) collective-permute-start(bf16[6,64,384]{2,0,1:T(8,128)(2,1)S(1)} %collective-permute-done.4), channel_id=1, source_target_pairs={{1,0},{2,1},{3,2},{4,3},{5,4},{6,5},{7,6},{0,7},{9,8},{10,9},{11,1... | collective-permute-start | bytes 884744 | tf_op jit(solution)/shard_map/ppermute | solution.py:30
  153.2 8.4 %collective-permute-start.3 = (bf16[6,64,384]{2,0,1:T(8,128)(2,1)S(1)}, bf16[6,64,384]{2,0,1:T(8,128)(2,1)S(1)}, u32[]{:S(2)}, u32[]{:S(2)}) collective-permute-start(bf16[6,64,384]{2,0,1:T(8,128)(2,1)S(1)} %collective-permute-done.2), channel_id=1, source_target_pairs={{0,1},{1,2},{2,3},{3,4},{4,5},{5,6},{6,7},{7,0},{8,9},{9,10},{10,1... | collective-permute-start | bytes 884744 | tf_op jit(solution)/shard_map/ppermute | solution.py:27
  157.2 11.9 %collective-permute-start.6 = (bf16[6,64,384]{2,0,1:T(8,128)(2,1)S(1)}, bf16[6,64,384]{2,0,1:T(8,128)(2,1)S(1)}, u32[]{:S(2)}, u32[]{:S(2)}) collective-permute-start(bf16[6,64,384]{2,0,1:T(8,128)(2,1)S(1)} %collective-permute-done.5), channel_id=1, source_target_pairs={{1,0},{2,1},{3,2},{4,3},{5,4},{6,5},{7,6},{0,7},{9,8},{10,9},{11,1... | collective-permute-start | bytes 884744 | tf_op jit(solution)/shard_map/ppermute | solution.py:30
  177.6 5.1 %copy-start.1 = (bf16[8,6,64,384]{3,1,2,0:T(8,128)(2,1)S(1)}, bf16[8,6,64,384]{3,1,2,0:T(8,128)(2,1)}, u32[]{:S(2)}) copy-start(bf16[8,6,64,384]{3,1,2,0:T(8,128)(2,1)} %gather_fusion.1) | copy-start | bytes 7077892
  205.1 5.9 %copy-start.2 = (f32[6,64,3072]{2,1,0:T(8,128)S(1)}, f32[6,64,3072]{2,1,0:T(8,128)}, u32[]{:S(2)}) copy-start(f32[6,64,3072]{2,1,0:T(8,128)} %reshape.343) | copy-start | bytes 14155780
  205.1 8.8 %copy-start.3 = (bf16[3072,384]{0,1:T(8,128)(2,1)S(1)}, bf16[3072,384]{0,1:T(8,128)(2,1)}, u32[]{:S(2)}) copy-start(bf16[3072,384]{0,1:T(8,128)(2,1)} %copy.55) | copy-start | bytes 7077892
  205.1 8.8 %copy-start.4 = (bf16[6,64,3072,1]{2,1,0,3:T(8,128)(2,1)S(1)}, bf16[6,64,3072,1]{2,1,0,3:T(8,128)(2,1)}, u32[]{:S(2)}) copy-start(bf16[6,64,3072,1]{2,1,0,3:T(8,128)(2,1)} %reshape.362) | copy-start | bytes 7077892
  210.9 4.7 %slice-start.2 = ((s8[5308416]{0:T(1024)(128)(4,1)}), s8[4194304]{0:T(1024)(128)(4,1)S(1)}, s32[]{:S(2)}) async-start(s8[5308416]{0:T(1024)(128)(4,1)} %bitcast.172), calls=%async_computation.4 | async-start | bytes 8388608
  213.9 1.7 slice-start.3
  223.1 19.8 %slice-start = ((s8[4718592]{0:T(1024)(128)(4,1)}), s8[524288]{0:T(1024)(128)(4,1)S(1)}, s32[]{:S(2)}) async-start(s8[4718592]{0:T(1024)(128)(4,1)} %bitcast.169), calls=%async_computation.2 | async-start | bytes 1048576
  232.4 10.5 %slice-start.1 = ((s8[4718592]{0:T(1024)(128)(4,1)}), s8[4194304]{0:T(1024)(128)(4,1)S(1)}, s32[]{:S(2)}) async-start(s8[4718592]{0:T(1024)(128)(4,1)} %bitcast.169), calls=%async_computation.3 | async-start | bytes 8388608
  232.4 10.5 %copy-start.5 = (bf16[3072,128]{1,0:T(8,128)(2,1)S(1)}, bf16[3072,128]{1,0:T(8,128)(2,1)}, u32[]{:S(2)}) copy-start(bf16[3072,128]{1,0:T(8,128)(2,1)} %param.17) | copy-start | bytes 2359300
  244.4 3.6 %copy-start.8 = (s32[6,8]{1,0:T(8,128)S(1)}, s32[6,8]{1,0:T(8,128)}, u32[]{:S(2)}) copy-start(s32[6,8]{1,0:T(8,128)} %param.23) | copy-start | bytes 580
Sparse Core Ops, SparseCore 0:
  10.6 104.8 all-gather.1
  248.1 75.3 all-reduce.1
